TPU v7x, 512 devices: a whole 4x8x8 slice. The times are simulated.
512 devices in a mesh: row: 32 (over y, x), col: 16 (over z, core).
Axes of the slice: x: 4, y: 8, z: 8, core: 2. Of those that a mesh axis runs over, the one named last changes fastest.
Arguments:
- tensor: float32 [512, 256, 2048], P(None, 'row', 'col'), may hold values from -60 to 60, as said below
- initial_basis: float32 [512, 128], replicated, may hold values from -6 to 6
Outputs:
- factor: float32 [512, 128], replicated
- core_tensor: float32 [128, 256, 2048], P(None, 'row', 'col')
Inputs may be any that keep to these rules, and one draw needn't show every extreme that they name: Entries of the data tensor.
All inputs are finite; a program needn't handle non-finite values.
Results may differ from a plain program's by a relative error of at most 0.00015.
Values sent between devices are 32-bit elements; how exact they have to be, the bound alone decides.
A program may use at most 64 MiB of HBM per device.

v0:
```python
import jax
import jax.numpy as jnp
from jax import lax
from jax.sharding import PartitionSpec as P

ITERS = 3


def gram_of(matrix):
    return lax.dot_general(
        matrix,
        matrix,
        (((1,), (1,)), ((), ())),
        precision=lax.Precision.HIGHEST,
        preferred_element_type=jnp.float32,
    )


def contract_rows(left_matrix, right_matrix):
    return lax.dot_general(
        left_matrix,
        right_matrix,
        (((0,), (0,)), ((), ())),
        precision=lax.Precision.HIGHEST,
        preferred_element_type=jnp.float32,
    )


def statistics(first_moment, second_moment, cell_count):
    average = first_moment / cell_count
    inverse_std = 1.0 / jnp.sqrt(second_moment / cell_count - average * average + 1e-05)
    return (average, inverse_std)


def local(tensor, initial_basis):
    variables = tensor.shape[0]
    fibres = tensor.reshape(variables, -1)
    cell_count = float(fibres.shape[1] * lax.axis_size("row") * lax.axis_size("col"))
    local_first = jnp.sum(fibres, axis=1)
    local_second = jnp.sum(fibres * fibres, axis=1)
    first_moment, second_moment = lax.psum((local_first, local_second), ("row", "col"))
    average, inverse_std = statistics(first_moment, second_moment, cell_count)
    normed = (fibres - average[:, None]) * inverse_std[:, None]
    gram_matrix = lax.psum(gram_of(normed), ("row", "col"))
    triangle = jnp.linalg.cholesky(gram_matrix)
    basis_cols = initial_basis
    for iteration in range(ITERS):
        projected = contract_rows(triangle, basis_cols)
        power_image = jnp.dot(
            triangle, projected, precision=lax.Precision.HIGHEST, preferred_element_type=jnp.float32
        )
        small_gram = contract_rows(power_image, power_image)
        small_factor = jnp.linalg.cholesky(small_gram)
        basis_cols = lax.linalg.triangular_solve(
            small_factor, power_image, left_side=False, lower=True, transpose_a=True
        )
    core_tensor = contract_rows(basis_cols, normed).reshape(
        basis_cols.shape[1], tensor.shape[1], tensor.shape[2]
    )
    return (basis_cols, core_tensor)


def solution(mesh):
    in_specs = (P(None, "row", "col"), P())
    out_specs = (P(), P(None, "row", "col"))
    return jax.shard_map(local, mesh=mesh, in_specs=in_specs, out_specs=out_specs, check_vma=False)
```

profile of v0, /device:TPU:1, one launch (start us, length us, event | category | flops | bytes accessed | tf_op | source)
XLA Modules:
  0.0 590.8 jit_solution(16528941097484791887)
XLA Ops:
  7.2 3.5 fusion.67
  10.7 106.1 %all-reduce.1 = (f32[512]{0:T(512)S(1)}, f32[512]{0:T(512)S(1)}) all-reduce(f32[512]{0:T(512)S(1)} %get-tuple-element.7, f32[512]{0:T(512)S(1)} %get-tuple-element.6), channel_id=1, replica_groups=mesh['row'=32,'col'=16] {'row','col'}, use_global_device_ids=true, to_apply=%region_3.0 | all-reduce | flops 1024 | bytes 8192 | tf_op jit(solution)/shard_map/psum | solution.py:41
  116.8 2.0 subtract_multiply_fusion
  118.8 4.9 fusion.4
  123.7 1.8 fusion.1
  125.5 2.1 copy.11
  127.6 264.8 %all-reduce.4.cloned.1.call-done = f32[512,512]{0,1:T(8,128)} async-done(((f32[512,512]{0,1:T(8,128)}), f32[512,512]{0,1:T(8,128)}) %all-reduce.4.cloned.1.call-update) | async-done | bytes 1048592 | tf_op jit(solution)/shard_map/psum | solution.py:44
  392.4 2.6 copy.7
  395.1 1.4 fusion.7
  397.5 11.7 %cholesky.120 = f32[128,128]{1,0:T(8,128)S(1)} custom-call(f32[128,128]{1,0:T(8,128)S(1)} %cholesky.356), custom_call_target="Cholesky" | custom-call | tf_op jit(solution)/shard_map/jit(cholesky)/cholesky | solution.py:45
  409.3 9.8 %custom-call.32 = f32[1,128,128]{1,2,0:T(8,128)S(1)} custom-call(f32[1,128,128]{2,1,0:T(8,128)S(1)} %get-tuple-element.19), custom_call_target="InvertDiagBlocksLowerTriangular" | custom-call | tf_op jit(solution)/shard_map/jit(cholesky)/cholesky | solution.py:45
  419.2 1.2 constant_dynamic-update-slice_fusion.2
  420.4 1.3 convolution_subtract_fusion
  422.4 11.7 %cholesky.244 = f32[128,128]{1,0:T(8,128)S(1)} custom-call(f32[128,128]{1,0:T(8,128)S(1)} %cholesky.360), custom_call_target="Cholesky" | custom-call | tf_op jit(solution)/shard_map/jit(cholesky)/cholesky | solution.py:45
  434.1 10.2 %custom-call.33 = f32[1,128,128]{1,2,0:T(8,128)S(1)} custom-call(f32[1,128,128]{2,1,0:T(8,128)S(1)} %get-tuple-element.16), custom_call_target="InvertDiagBlocksLowerTriangular" | custom-call | tf_op jit(solution)/shard_map/jit(cholesky)/cholesky | solution.py:45
  445.5 1.3 convolution_subtract_fusion.1
  447.4 13.2 %cholesky.265 = f32[128,128]{1,0:T(8,128)} custom-call(f32[128,128]{1,0:T(8,128)} %cholesky.365), custom_call_target="Cholesky" | custom-call | tf_op jit(solution)/shard_map/jit(cholesky)/cholesky | solution.py:45
  460.6 1.5 fusion.51
  462.8 11.3 %custom-call.34 = f32[1,128,128]{1,2,0:T(8,128)} custom-call(f32[1,128,128]{2,1,0:T(8,128)} %get-tuple-element.13), custom_call_target="InvertDiagBlocksLowerTriangular" | custom-call | tf_op jit(solution)/shard_map/jit(cholesky)/cholesky | solution.py:45
  475.2 1.2 convolution_subtract_fusion.2
  476.4 11.7 %cholesky.282 = f32[128,128]{1,0:T(8,128)S(1)} custom-call(f32[128,128]{1,0:T(8,128)S(1)} %convolution_subtract_fusion.2), custom_call_target="Cholesky" | custom-call | tf_op jit(solution)/shard_map/jit(cholesky)/cholesky | solution.py:45
  492.2 1.4 fusion.21
  496.6 12.5 %cholesky.325 = f32[128,128]{1,0:T(8,128)S(1)} custom-call(f32[128,128]{1,0:T(8,128)} %fusion.33), custom_call_target="Cholesky" | custom-call | tf_op jit(solution)/shard_map/jit(cholesky)/cholesky | solution.py:53
  510.5 9.8 %custom-call.37 = f32[1,128,128]{1,2,0:T(8,128)S(1)} custom-call(f32[1,128,128]{2,1,0:T(8,128)S(1)} %fusion.22), custom_call_target="InvertDiagBlocksLowerTriangular" | custom-call | tf_op jit(solution)/shard_map/triangular_solve/custom-call.8 | solution.py:54
  520.3 1.4 convolution_bitcast_fusion.1
  526.0 12.7 %cholesky.336 = f32[128,128]{1,0:T(8,128)S(1)} custom-call(f32[128,128]{1,0:T(8,128)} %fusion.31), custom_call_target="Cholesky" | custom-call | tf_op jit(solution)/shard_map/jit(cholesky)/cholesky | solution.py:53
  540.0 9.8 %custom-call.38 = f32[1,128,128]{1,2,0:T(8,128)S(1)} custom-call(f32[1,128,128]{2,1,0:T(8,128)S(1)} %fusion.23), custom_call_target="InvertDiagBlocksLowerTriangular" | custom-call | tf_op jit(solution)/shard_map/triangular_solve/custom-call.8 | solution.py:54
  549.8 1.4 convolution_bitcast_fusion
  554.8 11.9 %cholesky.347 = f32[128,128]{1,0:T(8,128)S(1)} custom-call(f32[128,128]{1,0:T(8,128)S(1)} %fusion.29), custom_call_target="Cholesky" | custom-call | tf_op jit(solution)/shard_map/jit(cholesky)/cholesky | solution.py:53
  568.0 9.8 %custom-call.39 = f32[1,128,128]{1,2,0:T(8,128)S(1)} custom-call(f32[1,128,128]{2,1,0:T(8,128)S(1)} %fusion.24), custom_call_target="InvertDiagBlocksLowerTriangular" | custom-call | tf_op jit(solution)/shard_map/triangular_solve/custom-call.8 | solution.py:54
  577.9 1.4 fusion.27
  579.2 2.3 fusion.9
  (56 shorter events, 23.6 us)
Async XLA Ops:
  7.2 485.0 %copy-start = (f32[512,128]{1,0:T(8,128)S(1)}, f32[512,128]{1,0:T(8,128)}, u32[]{:S(2)}) copy-start(f32[512,128]{1,0:T(8,128)} %param.6) | copy-start | bytes 786436
  7.2 109.6 %copy-start.1 = (f32[512,8,128]{2,1,0:T(8,128)S(1)}, f32[512,8,128]{2,1,0:T(8,128)}, u32[]{:S(2)}) copy-start(f32[512,8,128]{2,1,0:T(8,128)} %param.5) | copy-start | bytes 6291460
  7.2 385.2 %all-reduce.4.cloned.1.call-start = ((), (), s32[]{:S(2)}) async-start(), calls=%async_computation | async-start | bytes 2097152 | tf_op jit(solution)/shard_map/psum | solution.py:44
  392.4 2.6 copy-start.2
  396.5 1.0 copy-start.6
  421.7 0.7 copy-start.7
  494.6 0.7 copy-start.4
  523.9 0.7 copy-start.5
  553.4 0.7 copy-start.3
Sparse Core Ops, SparseCore 0:
  123.8 268.5 all-reduce.3
where the time goes:
time: 597 us; the launch traced here: 591 us
  waiting for transfers between devices  265 us (44%)
  other arithmetic  164 us (27%)
  blocking collectives  106 us (18%)
  matrix products  27 us (5%)
  between operations  17.5 us (3%)
  local copies, waits for them, and re-layouts  11.5 us (2%)
    psum x1, waiting for transfers between devices, local(): gram_matrix = lax.psum(gram_of(normed), ('row', 'col'))  265 us
    psum x1, blocking collectives, local(): lax.psum((local_first, local_second), ('row', 'col'))  106 us
    another operation x14, other arithmetic, local(): triangle = jnp.linalg.cholesky(gram_matrix)  83.3 us
    another operation x9, other arithmetic, local(): small_factor = jnp.linalg.cholesky(small_gram)  39.1 us
    another operation x6, other arithmetic, local(): lax.linalg.triangular_solve(small_factor, power_image, left_side=False, l...  31.4 us
  transfers between devices with their start and end apart: 1, of which 1 were waited for; matrix products, arithmetic and copies ran while one was open for 1% of the time, Pallas kernels for 0%

commit v1 on v0

v1 whole, which is shorter than its diff:
```python
import functools

import jax
import jax.numpy as jnp
from jax import lax
from jax.experimental import pallas as pl
from jax.experimental.pallas import tpu as pltpu
from jax.sharding import PartitionSpec as P

ITERS = 3
CHIPS_X = 4
BLOCK = 128
MESH = pl.DeviceIdType.MESH
SQUARES = ((1, 0), (2, 0), (3, 0), (0, 1), (2, 1), (3, 1), (3, 2), (2, 3))
PAIRED = (3, 7)


def ring_distance(step, extent):
    return min(step, extent - step)


def far_first(extent):
    return sorted(range(1, extent), key=lambda step: -ring_distance(step, extent))


def near_first(extent):
    return sorted(range(1, extent), key=lambda step: ring_distance(step, extent))


def dot_nt(left, right, precision=None):
    return lax.dot_general(
        left, right, (((1,), (1,)), ((), ())), precision=precision, preferred_element_type=jnp.float32
    )


def gram_kernel(
    sizes, cells,
    x_hbm, gram_ref, stats_ref,
    field, high, low, local, from_core, to_x, from_x, to_z, from_z, from_y, packed,
    load_sem, core_send, core_recv, x_send, x_recv, z_send, z_recv, y_send, y_recv,
    gz_send, gz_recv, gx_send, gx_recv, gc_send, gc_recv,
):
    nx, ny, nz = sizes
    tiles_x = 64 // nx
    tiles_z = tiles_x // nz
    row, col = lax.axis_index("row"), lax.axis_index("col")
    x, y = lax.rem(row, nx), lax.div(row, nx)
    core, z = lax.rem(col, 2), lax.div(col, 2)

    def device(dx=0, dy=0, dz=0, other=False):
        to_row = lax.rem(y + dy, ny) * nx + lax.rem(x + dx, nx)
        to_col = lax.rem(z + dz, nz) * 2 + (1 - core if other else core)
        return (to_row, to_col)

    peers = [device(other=True)]
    peers += [device(dx=d) for d in range(1, nx)]
    peers += [device(dz=d) for d in range(1, nz)]
    peers += [device(dy=d) for d in range(1, ny)]
    barrier = pltpu.get_barrier_semaphore()
    for peer in peers:
        pl.semaphore_signal(barrier, inc=1, device_id=peer, device_id_type=MESH)

    def send(src, dst, send_sem, recv_sem, peer):
        copy = pltpu.make_async_remote_copy(
            src_ref=src, dst_ref=dst, send_sem=send_sem, recv_sem=recv_sem,
            device_id=peer, device_id_type=MESH,
        )
        copy.start()
        return copy

    load = pltpu.make_async_copy(x_hbm, field, load_sem)
    load.start()
    load.wait()

    rows = field.shape[0]
    slabs = field.shape[1]
    width = float(slabs * BLOCK)
    blocks = rows // BLOCK
    below = lax.broadcasted_iota(jnp.int32, (BLOCK, BLOCK), 0)
    across = lax.broadcasted_iota(jnp.int32, (BLOCK, BLOCK), 1)
    on_diagonal = below == across

    mean_down, mean_over, sums = [], [], []
    for b in range(blocks):
        here = pl.ds(b * BLOCK, BLOCK)
        total = field[here, 0, :]
        for s in range(1, slabs):
            total = total + field[here, s, :]
        total = jnp.broadcast_to(jnp.sum(total, axis=1, keepdims=True), (BLOCK, BLOCK))
        mean = total * (1.0 / width)
        for s in range(slabs):
            centred = field[here, s, :] - mean
            top = centred.astype(jnp.bfloat16)
            high[here, pl.ds(s * BLOCK, BLOCK)] = top
            low[here, pl.ds(s * BLOCK, BLOCK)] = (centred - top.astype(jnp.float32)).astype(jnp.bfloat16)
        turned = total.T
        mean_down.append(mean)
        mean_over.append(turned * (1.0 / width))
        sums.append(turned[0:1, :])

    pair = 2 * BLOCK
    square = {}
    for bi in range(blocks // 2):
        for bj in range(bi + 1):
            left, right = pl.ds(bi * pair, pair), pl.ds(bj * pair, pair)
            value = dot_nt(high[left, :], high[right, :])
            value = value + dot_nt(high[left, :], low[right, :])
            value = value + dot_nt(low[left, :], high[right, :])
            for i in range(2):
                for j in range(2):
                    r, q = 2 * bi + i, 2 * bj + j
                    if r >= q:
                        square[r, q] = value[i * BLOCK:(i + 1) * BLOCK, j * BLOCK:(j + 1) * BLOCK] + (
                            width * mean_down[r] * mean_over[q]
                        )

    def diagonal_of(block):
        return jnp.sum(jnp.where(on_diagonal, block, 0.0), axis=0, keepdims=True)

    extra = jnp.concatenate(
        sums + [diagonal_of(square[0, 0]), diagonal_of(square[2, 2]), jnp.zeros((2, BLOCK), jnp.float32)], axis=0
    )
    for index, (r, q) in enumerate(SQUARES):
        half, slot = index // 4, (index % 4) * 16
        if index in PAIRED:
            first, second = min(r, q), max(r, q)
            block = jnp.where(below > across, square[first, first], square[second, second])
        else:
            block = square[r, q]
        local[half, slot // tiles_x, pl.ds(slot % tiles_x, 16)] = block.reshape(16, 8, BLOCK)
    for half in range(2):
        for piece in range(nx):
            local[half, piece, tiles_x] = extra

    pl.semaphore_wait(barrier, len(peers))

    order_x = far_first(nx) + [0]
    partner = device(other=True)
    sent = []
    core_copies = {}
    for d in order_x:
        core_copies[d] = send(
            local.at[1 - core, lax.rem(x + d, nx)], from_core.at[d], core_send.at[d], core_recv.at[d], partner
        )
    sent += list(core_copies.values())
    x_copies = {}
    for d in order_x:
        core_copies[d].wait_recv()
        value = local[core, lax.rem(x + d, nx)] + from_core[d]
        if d == 0:
            from_x[0] = value
        else:
            to_x[d - 1] = value
            x_copies[d] = send(to_x.at[d - 1], from_x.at[d], x_send.at[d - 1], x_recv.at[d - 1], device(dx=d))
    sent += list(x_copies.values())
    for d in near_first(nx):
        x_copies[d].wait_recv()

    def x_sum(window):
        value = from_x[lax.rem(x + nx, nx), window]
        for j in range(1, nx):
            value = value + from_x[lax.rem(x + nx - j, nx), window]
        return value

    moments = x_sum(pl.ds(tiles_x, 1))
    z_copies = {}
    for d in far_first(nz) + [0]:
        value = x_sum(pl.ds(lax.rem(z + d, nz) * tiles_z, tiles_z))
        if d == 0:
            from_z[0, pl.ds(0, tiles_z)] = value
            from_z[0, pl.ds(tiles_z, 1)] = moments
        else:
            to_z[d - 1, pl.ds(0, tiles_z)] = value
            to_z[d - 1, pl.ds(tiles_z, 1)] = moments
            z_copies[d] = send(to_z.at[d - 1], from_z.at[d], z_send.at[d - 1], z_recv.at[d - 1], device(dz=d))
    sent += list(z_copies.values())
    for d in near_first(nz):
        z_copies[d].wait_recv()
    value = from_z[z]
    for j in range(1, nz):
        value = value + from_z[lax.rem(z + nz - j, nz)]
    from_y[0] = value
    y_copies = {}
    for d in far_first(ny):
        y_copies[d] = send(from_y.at[0], from_y.at[d], y_send.at[d - 1], y_recv.at[d - 1], device(dy=d))
    sent += list(y_copies.values())
    for d in near_first(ny):
        y_copies[d].wait_recv()
    value = from_y[y]
    for j in range(1, ny):
        value = value + from_y[lax.rem(y + ny - j, ny)]

    def place(dx, dz):
        tile = 64 * core + tiles_x * lax.rem(x + nx - dx, nx) + tiles_z * lax.rem(z + nz - dz, nz)
        return packed.at[pl.ds(tile, tiles_z)]

    packed[pl.ds(64 * core + tiles_x * x + tiles_z * z, tiles_z)] = value[0:tiles_z]
    extra = value[tiles_z]

    gz, gx, gc = {}, {}, {}
    mine = place(0, 0)
    for d in far_first(nz):
        gz[d] = send(mine, mine, gz_send.at[d - 1], gz_recv.at[d - 1], device(dz=d))

    def pass_on(dx, dz):
        piece = place(dx, dz)
        if dx == 0:
            for d in far_first(nx):
                gx[d, dz] = send(piece, piece, gx_send.at[d - 1, dz], gx_recv.at[d - 1, dz], device(dx=d))
        gc[dx, dz] = send(piece, piece, gc_send.at[dx, dz], gc_recv.at[dx, dz], partner)

    pass_on(0, 0)
    arrivals = [(1.0 + ring_distance(d, nz), 0, d) for d in range(1, nz)]
    arrivals += [
        ((1.0 + ring_distance(d, nz) if d else 0.0) + 1.0 + ring_distance(e, nx), e, d)
        for e in range(1, nx) for d in range(nz)
    ]
    for _, e, d in sorted(arrivals):
        if e == 0:
            gz[d].wait_recv()
        else:
            gx[e, d].wait_recv()
        pass_on(e, d)
    for copy in gc.values():
        copy.wait_recv()

    means, scales, seconds = [], [], []
    def matrix(index):
        return packed[pl.ds(16 * index, 16)].reshape(BLOCK, BLOCK)

    whole = {}
    for index, (r, q) in enumerate(SQUARES):
        block = matrix(index)
        if index in PAIRED:
            first, second = min(r, q), max(r, q)
            turned = block.T
            line = extra[4 + first // 2:5 + first // 2, :]
            whole[first, first] = jnp.where(
                below > across, block, jnp.where(below < across, turned, jnp.broadcast_to(line, (BLOCK, BLOCK)))
            )
            whole[second, second] = jnp.where(below <= across, block, turned)
        else:
            whole[r, q] = block
    for b in range(blocks):
        average = extra[b:b + 1, :] / cells
        if b % 2 == 0:
            second = extra[4 + b // 2:5 + b // 2, :]
        else:
            second = diagonal_of(whole[b, b])
        scale = 1.0 / jnp.sqrt(second / cells - average * average + 1e-05)
        stats_ref[b:b + 1, :] = average
        stats_ref[4 + b:5 + b, :] = scale
        means.append(jnp.broadcast_to(average, (BLOCK, BLOCK)))
        scales.append(jnp.broadcast_to(scale, (BLOCK, BLOCK)))
    means_down = [value.T for value in means]
    scales_down = [value.T for value in scales]
    for (r, q), block in whole.items():
        value = (block - cells * (means_down[r] * means[q])) * scales_down[r] * scales[q]
        gram_ref[pl.ds(r * BLOCK, BLOCK), pl.ds(q * BLOCK, BLOCK)] = value
        if r != q:
            gram_ref[pl.ds(q * BLOCK, BLOCK), pl.ds(r * BLOCK, BLOCK)] = value.T

    for copy in sent + list(gz.values()) + list(gx.values()) + list(gc.values()):
        copy.wait_send()


def gram_call(tensor, sizes, cells):
    nx, ny, nz = sizes
    rows, slabs, lanes = tensor.shape
    tiles_x = 64 // nx
    tiles_z = tiles_x // nz
    f32, bf16 = jnp.float32, jnp.bfloat16
    vmem = pltpu.VMEM
    dma = pltpu.SemaphoreType.DMA
    return pl.pallas_call(
        functools.partial(gram_kernel, sizes, cells),
        out_shape=(
            jax.ShapeDtypeStruct((rows, rows), f32),
            jax.ShapeDtypeStruct((8, lanes), f32),
        ),
        in_specs=[pl.BlockSpec(memory_space=pl.ANY)],
        out_specs=(pl.BlockSpec(memory_space=pltpu.VMEM), pl.BlockSpec(memory_space=pltpu.VMEM)),
        scratch_shapes=[
            vmem((rows, slabs, lanes), f32),
            vmem((rows, slabs * lanes), bf16),
            vmem((rows, slabs * lanes), bf16),
            vmem((2, nx, tiles_x + 1, 8, lanes), f32),
            vmem((nx, tiles_x + 1, 8, lanes), f32),
            vmem((nx - 1, tiles_x + 1, 8, lanes), f32),
            vmem((nx, tiles_x + 1, 8, lanes), f32),
            vmem((nz - 1, tiles_z + 1, 8, lanes), f32),
            vmem((nz, tiles_z + 1, 8, lanes), f32),
            vmem((ny, tiles_z + 1, 8, lanes), f32),
            vmem((128, 8, lanes), f32),
            dma,
            dma((nx,)), dma((nx,)),
            dma((nx - 1,)), dma((nx - 1,)),
            dma((nz - 1,)), dma((nz - 1,)),
            dma((ny - 1,)), dma((ny - 1,)),
            dma((nz - 1,)), dma((nz - 1,)),
            dma((nx - 1, nz)), dma((nx - 1, nz)),
            dma((nx, nz)), dma((nx, nz)),
        ],
        compiler_params=pltpu.CompilerParams(collective_id=0, has_side_effects=True),
    )(tensor)


def contract_rows(left_matrix, right_matrix):
    return lax.dot_general(
        left_matrix,
        right_matrix,
        (((0,), (0,)), ((), ())),
        precision=lax.Precision.HIGHEST,
        preferred_element_type=jnp.float32,
    )


def local_step(sizes, tensor, initial_basis):
    rows = tensor.shape[0]
    cells = float(tensor.shape[1] * tensor.shape[2] * lax.axis_size("row") * lax.axis_size("col"))
    gram_matrix, stats = gram_call(tensor, sizes, cells)
    average, inverse_std = stats[0:4].reshape(rows), stats[4:8].reshape(rows)
    basis_cols = initial_basis
    for iteration in range(ITERS):
        power_image = jnp.dot(
            gram_matrix, basis_cols, precision=lax.Precision.HIGHEST, preferred_element_type=jnp.float32
        )
        small_gram = contract_rows(power_image, power_image)
        small_factor = jnp.linalg.cholesky(small_gram)
        basis_cols = lax.linalg.triangular_solve(
            small_factor, power_image, left_side=False, lower=True, transpose_a=True
        )
    normed = (tensor - average[:, None, None]) * inverse_std[:, None, None]
    core_tensor = lax.dot_general(
        basis_cols, normed, (((0,), (0,)), ((), ())),
        precision=lax.Precision.HIGHEST, preferred_element_type=jnp.float32,
    )
    return (basis_cols, core_tensor)


def solution(mesh):
    nx = CHIPS_X
    sizes = (nx, mesh.shape["row"] // nx, mesh.shape["col"] // 2)
    in_specs = (P(None, "row", "col"), P())
    out_specs = (P(), P(None, "row", "col"))
    return jax.shard_map(
        functools.partial(local_step, sizes), mesh=mesh, in_specs=in_specs, out_specs=out_specs, check_vma=False
    )
```

time: 597 us -> 136 us (0.23); the launches traced: 591 us -> 136 us
  waiting for transfers between devices: 265 us -> 0 us
  blocking collectives: 106 us -> 0 us
  other arithmetic: 164 us -> 72.4 us
  Pallas kernels: 0 us -> 48.7 us
  between operations: 17.5 us -> 0.9 us
  matrix products: 27 us -> 10.7 us
  local copies, waits for them, and re-layouts: 11.5 us -> 3.24 us
    psum x1 -> x0, waiting for transfers between devices: 265 us -> none  [local(): gram_matrix = lax.psum(gram_of(normed), ('row', 'col'))]
    psum x1 -> x0, blocking collectives: 106 us -> none  [local(): lax.psum((local_first, local_second), ('row', 'col'))]
    another operation x29 -> x15, other arithmetic: 154 us -> 69.7 us  [the longest x9 38.2 us: local_step(): small_factor = jnp.linalg.cholesky(small_gram)]
    pallas_call x0 -> x1, Pallas kernels: none -> 48.7 us  [gram_call(): pl.pallas_call(functools.partial(gram_kernel, sizes, cells), out_shape=(j...]
    another operation x9 -> x3, matrix products: 11.3 us -> 3.16 us  [local_step(): lax.linalg.triangular_solve(small_factor, power_image, left_side=False, l...]
    dot_general x7 -> x3, matrix products: 7.87 us -> 1.35 us  [contract_rows(): lax.dot_general(left_matrix, right_matrix, (((0,), (0,)), ((), ())), prec...]
  transfers between devices with their start and end apart: 1 -> 0, of which waited for: 1 -> 0; matrix products, arithmetic and copies ran while one was open for 1% -> 0% of each run, Pallas kernels for 0% -> 0%
where the time goes in v1:
time: 136 us
  other arithmetic  72.4 us (53%)
  Pallas kernels  48.7 us (36%)
  matrix products  10.7 us (8%)
  local copies, waits for them, and re-layouts  3.24 us (2%)
    pallas_call x1, Pallas kernels, gram_call(): pl.pallas_call(functools.partial(gram_kernel, sizes, cells), out_shape=(j...  48.7 us
    another operation x9, other arithmetic, local_step(): small_factor = jnp.linalg.cholesky(small_gram)  38.2 us
    another operation x6, other arithmetic, local_step(): lax.linalg.triangular_solve(small_factor, power_image, left_side=False, l...  31.5 us
    dot_general x3, matrix products, local_step(): jnp.dot(gram_matrix, basis_cols, precision=lax.Precision.HIGHEST, preferr...  4.64 us
    another operation x3, matrix products, local_step(): lax.linalg.triangular_solve(small_factor, power_image, left_side=False, l...  3.16 us
    unnamed x14, local copies, waits for them, and re-layouts  2.97 us

profile of v1, /device:TPU:1, one launch (start us, length us, event | category | flops | bytes accessed | tf_op | source)
XLA Modules:
  0.0 136.0 jit_solution(18124371702832785662)
XLA Ops:
  0.6 48.7 %shard_map.41 = (f32[512,512]{1,0:T(8,128)}, f32[8,128]{1,0:T(8,128)}) custom-call(f32[512,8,128]{2,1,0:T(8,128)} %x_hbm.1), custom_call_target="tpu_custom_call" | custom-call | tf_op jit(solution)/shard_map/pallas_call | solution.py:275
  49.4 2.3 %fusion.19 = f32[512,128]{1,0:T(8,128)S(1)} fusion(f32[512,512]{1,0:T(8,128)} %get-tuple-element.6, f32[512,128]{1,0:T(8,128)S(1)} %copy-done), kind=kOutput, calls=%fused_computation.36 | convolution fusion | flops 402653184 | bytes 1572864 | tf_op jit(solution)/shard_map/dot_general | solution.py:325
  51.7 0.6 fusion.20
  52.3 0.1 copy.4
  52.4 11.7 %cholesky.59 = f32[128,128]{1,0:T(8,128)S(1)} custom-call(f32[128,128]{1,0:T(8,128)S(1)} %fusion.14), custom_call_target="Cholesky" | custom-call | tf_op jit(solution)/shard_map/jit(cholesky)/cholesky | solution.py:329
  64.2 0.6 compare_reduce_fusion.2
  64.8 0.7 fusion.6
  65.5 10.0 %custom-call.7 = f32[1,128,128]{1,2,0:T(8,128)S(1)} custom-call(f32[1,128,128]{2,1,0:T(8,128)S(1)} %fusion.6), custom_call_target="InvertDiagBlocksLowerTriangular" | custom-call | tf_op jit(solution)/shard_map/triangular_solve/custom-call.0 | solution.py:330
  75.4 0.4 convolution_bitcast_fusion.1
  75.9 1.2 fusion.21
  77.1 0.4 fusion.22
  77.4 0.3 copy-done.4
  77.7 0.1 copy.5
  77.9 0.6 fusion.12
  78.5 12.6 %cholesky.70 = f32[128,128]{1,0:T(8,128)S(1)} custom-call(f32[128,128]{1,0:T(8,128)} %fusion.12), custom_call_target="Cholesky" | custom-call | tf_op jit(solution)/shard_map/jit(cholesky)/cholesky | solution.py:329
  91.1 0.6 compare_reduce_fusion.1
  91.8 0.7 fusion.7
  92.4 9.8 %custom-call.8 = f32[1,128,128]{1,2,0:T(8,128)S(1)} custom-call(f32[1,128,128]{2,1,0:T(8,128)S(1)} %fusion.7), custom_call_target="InvertDiagBlocksLowerTriangular" | custom-call | tf_op jit(solution)/shard_map/triangular_solve/custom-call.0 | solution.py:330
  102.2 1.4 %convolution_bitcast_fusion = f32[512,128]{0,1:T(8,128)S(1)} fusion(f32[128,512]{1,0:T(8,128)} %copy-done.4, f32[1,128,128]{1,2,0:T(8,128)S(1)} %custom-call.8), kind=kOutput, calls=%fused_computation.3 | convolution fusion | flops 100663296 | bytes 589824 | tf_op jit(solution)/shard_map/triangular_solve/dot.3 | solution.py:330
  103.6 1.2 fusion.23
  104.8 0.7 copy-done.3
  105.5 0.4 fusion.24
  105.9 0.1 copy.6
  106.0 11.9 %cholesky.81 = f32[128,128]{1,0:T(8,128)S(1)} custom-call(f32[128,128]{1,0:T(8,128)S(1)} %fusion.10), custom_call_target="Cholesky" | custom-call | tf_op jit(solution)/shard_map/jit(cholesky)/cholesky | solution.py:329
  117.9 0.6 compare_reduce_fusion
  118.6 0.7 fusion.8
  119.2 9.8 %custom-call.9 = f32[1,128,128]{1,2,0:T(8,128)S(1)} custom-call(f32[1,128,128]{2,1,0:T(8,128)S(1)} %fusion.8), custom_call_target="InvertDiagBlocksLowerTriangular" | custom-call | tf_op jit(solution)/shard_map/triangular_solve/custom-call.0 | solution.py:330
  129.1 1.4 %fusion.3 = f32[128,512]{1,0:T(8,128)S(1)} fusion(f32[128,512]{1,0:T(8,128)} %copy-done.3, f32[1,128,128]{1,2,0:T(8,128)S(1)} %custom-call.9), kind=kOutput, calls=%fused_computation.6 | convolution fusion | flops 100663296 | bytes 589824 | tf_op jit(solution)/shard_map/triangular_solve/dot.3 | solution.py:330
  130.5 2.0 %subtract_multiply_fusion = f32[512,8,128]{2,1,0:T(8,128)S(1)} fusion(f32[512,8,128]{2,1,0:T(8,128)S(1)} %copy-done.2, f32[512]{0:T(512)S(1)} %get-tuple-element.11, f32[512]{0:T(512)S(1)} %get-tuple-element.10), kind=kLoop, calls=%fused_computation.2 | loop fusion | flops 1048576 | bytes 4198400 | tf_op jit(solution)/shard_map/mul | solution.py:333
  132.5 1.6 %fusion = f32[128,8,128]{2,0,1:T(8,128)S(1)} fusion(f32[512,8,128]{2,1,0:T(8,128)S(1)} %subtract_multiply_fusion, f32[128,512]{1,0:T(8,128)S(1)} %fusion.3), kind=kOutput, calls=%fused_computation | convolution fusion | flops 805306368 | bytes 2883584 | tf_op jit(solution)/shard_map/dot_general | solution.py:334
  134.0 1.1 copy.9
  135.1 0.8 copy.8
  (16 shorter events, 0.2 us)
Async XLA Ops:
  0.6 48.8 %copy-start = (f32[512,128]{1,0:T(8,128)S(1)}, f32[512,128]{1,0:T(8,128)}, u32[]{:S(2)}) copy-start(f32[512,128]{1,0:T(8,128)} %param.6) | copy-start | bytes 786436
  49.4 26.5 %copy-start.1 = (f32[512,512]{1,0:T(8,128)S(1)}, f32[512,512]{1,0:T(8,128)}, u32[]{:S(2)}) copy-start(f32[512,512]{1,0:T(8,128)} %get-tuple-element.6) | copy-start | bytes 3145732
  77.0 0.7 copy-start.4
  77.8 52.6 %copy-start.5 = (f32[8,128]{1,0:T(8,128)S(1)}, f32[8,128]{1,0:T(8,128)}, u32[]{:S(2)}) copy-start(f32[8,128]{1,0:T(8,128)} %get-tuple-element.7) | copy-start | bytes 12292
  77.9 52.6 %copy-start.2 = (f32[512,8,128]{2,1,0:T(8,128)S(1)}, f32[512,8,128]{2,1,0:T(8,128)}, u32[]{:S(2)}) copy-start(f32[512,8,128]{2,1,0:T(8,128)} %x_hbm.1) | copy-start | bytes 6291460
  104.8 0.7 copy-start.3

commit v2 on v1

--- a/solution.py
+++ b/solution.py
@@ -35,8 +35,8 @@
 
 def gram_kernel(
     sizes, cells,
-    x_hbm, gram_ref, stats_ref,
-    field, high, low, local, from_core, to_x, from_x, to_z, from_z, from_y, packed,
+    x_hbm, gram_ref, stats_ref, high, low,
+    field, local, from_core, to_x, from_x, to_z, from_z, from_y, packed,
     load_sem, core_send, core_recv, x_send, x_recv, z_send, z_recv, y_send, y_recv,
     gz_send, gz_recv, gx_send, gx_recv, gc_send, gc_recv,
 ):
@@ -250,12 +250,14 @@
         scale = 1.0 / jnp.sqrt(second / cells - average * average + 1e-05)
         stats_ref[b:b + 1, :] = average
         stats_ref[4 + b:5 + b, :] = scale
+        stats_ref[8 + b:9 + b, :] = sums[b] * (1.0 / width) - average
         means.append(jnp.broadcast_to(average, (BLOCK, BLOCK)))
         scales.append(jnp.broadcast_to(scale, (BLOCK, BLOCK)))
+    stats_ref[16:24, :] = jnp.ones((8, BLOCK), jnp.float32)
     means_down = [value.T for value in means]
     scales_down = [value.T for value in scales]
     for (r, q), block in whole.items():
-        value = (block - cells * (means_down[r] * means[q])) * scales_down[r] * scales[q]
+        value = (block * (1.0 / cells) - means_down[r] * means[q]) * scales_down[r] * scales[q]
         gram_ref[pl.ds(r * BLOCK, BLOCK), pl.ds(q * BLOCK, BLOCK)] = value
         if r != q:
             gram_ref[pl.ds(q * BLOCK, BLOCK), pl.ds(r * BLOCK, BLOCK)] = value.T
@@ -276,14 +278,14 @@
         functools.partial(gram_kernel, sizes, cells),
         out_shape=(
             jax.ShapeDtypeStruct((rows, rows), f32),
-            jax.ShapeDtypeStruct((8, lanes), f32),
+            jax.ShapeDtypeStruct((24, lanes), f32),
+            jax.ShapeDtypeStruct((rows, slabs * lanes), bf16),
+            jax.ShapeDtypeStruct((rows, slabs * lanes), bf16),
         ),
         in_specs=[pl.BlockSpec(memory_space=pl.ANY)],
-        out_specs=(pl.BlockSpec(memory_space=pltpu.VMEM), pl.BlockSpec(memory_space=pltpu.VMEM)),
+        out_specs=(pl.BlockSpec(memory_space=pltpu.VMEM),) * 4,
         scratch_shapes=[
             vmem((rows, slabs, lanes), f32),
-            vmem((rows, slabs * lanes), bf16),
-            vmem((rows, slabs * lanes), bf16),
             vmem((2, nx, tiles_x + 1, 8, lanes), f32),
             vmem((nx, tiles_x + 1, 8, lanes), f32),
             vmem((nx - 1, tiles_x + 1, 8, lanes), f32),
@@ -305,37 +307,157 @@
     )(tensor)
 
 
-def contract_rows(left_matrix, right_matrix):
-    return lax.dot_general(
-        left_matrix,
-        right_matrix,
-        (((0,), (0,)), ((), ())),
-        precision=lax.Precision.HIGHEST,
-        preferred_element_type=jnp.float32,
-    )
+def over(value, lane, one):
+    return jnp.broadcast_to(value[:, lane:lane + 1], (8, BLOCK)) * one
+
+
+def down(value, line):
+    return jnp.broadcast_to(value[line:line + 1, :], (8, BLOCK))
+
+
+def add_up(terms):
+    while len(terms) > 1:
+        terms = [terms[i] + terms[i + 1] for i in range(0, len(terms), 2)]
+    return terms[0]
+
+
+def inverse_factor(matrix, one):
+    groups = BLOCK // 8
+    line = lax.broadcasted_iota(jnp.int32, (8, BLOCK), 0)
+    lane = lax.broadcasted_iota(jnp.int32, (8, BLOCK), 1)
+    a = [matrix[8 * v:8 * v + 8, :] for v in range(groups)]
+    w = [jnp.where(lane == line + 8 * v, 1.0, 0.0).astype(jnp.float32) for v in range(groups)]
+    result = []
+    panel = [over(a[0], m, one) for m in range(8)]
+    under = [over(a[1], m, one) for m in range(8)]
+    for v0 in range(groups):
+        first = 8 * v0
+        more = v0 + 1 < groups
+        if more:
+            ahead = [over(a[v0 + 1], first + 8 + m, one) for m in range(8)]
+            spread = [under] + [
+                [over(a[v], first + m, one) for m in range(8)] for v in range(v0 + 2, groups)
+            ]
+            rest = list(under)
+        row_a, row_w = a[v0], w[v0]
+        ratios = []
+        for j in range(8):
+            pivot = down(panel[j], j)
+            reciprocal = 1.0 / pivot
+            pivots = pivot if j == 0 else jnp.where(line == j, pivot, pivots)
+            reciprocals = reciprocal if j == 0 else jnp.where(line == j, reciprocal, reciprocals)
+            if more:
+                ratios.append(rest[j] * reciprocal)
+            if j < 7:
+                ratio = jnp.where(line > j, panel[j] * reciprocal, 0.0)
+                for m in range(j + 1, 8):
+                    entry = down(panel[m], j)
+                    panel[m] = panel[m] - ratio * entry
+                    if more:
+                        rest[m] = rest[m] - ratios[j] * entry
+                row_a = row_a - ratio * down(row_a, j)
+                row_w = row_w - ratio * down(row_w, j)
+        result.append(row_w * lax.rsqrt(pivots))
+        if more:
+            following = [
+                ahead[m] - add_up([ratios[j] * down(rest[j], m) for j in range(8)]) for m in range(8)
+            ]
+            row_a, row_w = row_a * reciprocals, row_w * reciprocals
+            for j in range(7, 0, -1):
+                ratio = jnp.where(line < j, panel[j] * reciprocals, 0.0)
+                row_a = row_a - ratio * down(row_a, j)
+                row_w = row_w - ratio * down(row_w, j)
+            from_a = [down(row_a, m) for m in range(8)]
+            from_w = [down(row_w, m) for m in range(8)]
+            for index, v in enumerate(range(v0 + 1, groups)):
+                a[v] = a[v] - add_up([spread[index][m] * from_a[m] for m in range(8)])
+                w[v] = w[v] - add_up([spread[index][m] * from_w[m] for m in range(8)])
+            panel = following
+            if v0 + 2 < groups:
+                under = [over(a[v0 + 2], first + 8 + m, one) for m in range(8)]
+    return result
+
+
+def split(value):
+    top = value.astype(jnp.bfloat16)
+    return top, (value - top.astype(jnp.float32)).astype(jnp.bfloat16)
+
+
+def basis_kernel(gram_ref, stats_ref, basis_ref, high_hbm, low_hbm, factor_ref, core_ref, high, low, turned, image, inverse, sems):
+    loads = [
+        pltpu.make_async_copy(high_hbm, high, sems.at[0]),
+        pltpu.make_async_copy(low_hbm, low, sems.at[1]),
+    ]
+    for load in loads:
+        load.start()
+    rows, rank = basis_ref.shape
+    blocks = rows // BLOCK
+    highest = lax.Precision.HIGHEST
+    for b in range(blocks):
+        turned[:, b * BLOCK:(b + 1) * BLOCK] = basis_ref[pl.ds(b * BLOCK, BLOCK), :].T
+    one = stats_ref[16:24, :]
+
+    def body(iteration, carry):
+        image[...] = jnp.dot(turned[...], gram_ref[...], precision=highest, preferred_element_type=jnp.float32)
+        small = dot_nt(image[...], image[...], precision=highest)
+        for v, group in enumerate(inverse_factor(small, one)):
+            inverse[pl.ds(8 * v, 8), :] = group
+        turned[...] = jnp.dot(inverse[...], image[...], precision=highest, preferred_element_type=jnp.float32)
+        return carry
+
+    lax.fori_loop(0, ITERS, body, 0)
+
+    constant = None
+    for b in range(blocks):
+        window = pl.ds(b * BLOCK, BLOCK)
+        value = turned[:, window]
+        factor_ref[window, :] = value.T
+        value = value * stats_ref[4 + b:5 + b, :]
+        image[:, window] = value
+        term = value * stats_ref[8 + b:9 + b, :]
+        constant = term if constant is None else constant + term
+    constant = jnp.broadcast_to(jnp.sum(constant, axis=1, keepdims=True), (rank, BLOCK))
+    top, rest = split(image[...])
+    for load in loads:
+        load.wait()
+    slabs = core_ref.shape[1]
+    for s in range(0, slabs, 2):
+        window = pl.ds(s * BLOCK, 2 * BLOCK)
+        value = jnp.dot(top, high[:, window], preferred_element_type=jnp.float32)
+        value = value + jnp.dot(top, low[:, window], preferred_element_type=jnp.float32)
+        value = value + jnp.dot(rest, high[:, window], preferred_element_type=jnp.float32)
+        core_ref[:, s, :] = value[:, :BLOCK] + constant
+        core_ref[:, s + 1, :] = value[:, BLOCK:] + constant
+
+
+def basis_call(gram_matrix, stats, basis, high, low, slabs):
+    rows, rank = basis.shape
+    f32, bf16 = jnp.float32, jnp.bfloat16
+    vmem = pl.BlockSpec(memory_space=pltpu.VMEM)
+    hbm = pl.BlockSpec(memory_space=pl.ANY)
+    return pl.pallas_call(
+        basis_kernel,
+        out_shape=(
+            jax.ShapeDtypeStruct((rows, rank), f32),
+            jax.ShapeDtypeStruct((rank, slabs, BLOCK), f32),
+        ),
+        in_specs=[vmem, vmem, vmem, hbm, hbm],
+        out_specs=(vmem, vmem),
+        scratch_shapes=[
+            pltpu.VMEM(high.shape, bf16),
+            pltpu.VMEM(low.shape, bf16),
+            pltpu.VMEM((rank, rows), f32),
+            pltpu.VMEM((rank, rows), f32),
+            pltpu.VMEM((rank, rank), f32),
+            pltpu.SemaphoreType.DMA((2,)),
+        ],
+    )(gram_matrix, stats, basis, high, low)
 
 
 def local_step(sizes, tensor, initial_basis):
-    rows = tensor.shape[0]
     cells = float(tensor.shape[1] * tensor.shape[2] * lax.axis_size("row") * lax.axis_size("col"))
-    gram_matrix, stats = gram_call(tensor, sizes, cells)
-    average, inverse_std = stats[0:4].reshape(rows), stats[4:8].reshape(rows)
-    basis_cols = initial_basis
-    for iteration in range(ITERS):
-        power_image = jnp.dot(
-            gram_matrix, basis_cols, precision=lax.Precision.HIGHEST, preferred_element_type=jnp.float32
-        )
-        small_gram = contract_rows(power_image, power_image)
-        small_factor = jnp.linalg.cholesky(small_gram)
-        basis_cols = lax.linalg.triangular_solve(
-            small_factor, power_image, left_side=False, lower=True, transpose_a=True
-        )
-    normed = (tensor - average[:, None, None]) * inverse_std[:, None, None]
-    core_tensor = lax.dot_general(
-        basis_cols, normed, (((0,), (0,)), ((), ())),
-        precision=lax.Precision.HIGHEST, preferred_element_type=jnp.float32,
-    )
-    return (basis_cols, core_tensor)
+    gram_matrix, stats, high, low = gram_call(tensor, sizes, cells)
+    return basis_call(gram_matrix, stats, initial_basis, high, low, tensor.shape[1])
 
 
 def solution(mesh):

time: 136 us -> 66.1 us (0.49)
  other arithmetic: 72.4 us -> 0 us
  Pallas kernels: 48.7 us -> 65.3 us
  matrix products: 10.7 us -> 0 us
  local copies, waits for them, and re-layouts: 3.24 us -> 0 us
    another operation x15 -> x0, other arithmetic: 69.7 us -> none  [the longest x9 38.2 us: local_step(): small_factor = jnp.linalg.cholesky(small_gram)]
    pallas_call x0 -> x1, Pallas kernels: none -> 16 us  [basis_call(): pl.pallas_call(basis_kernel, out_shape=(jax.ShapeDtypeStruct((rows, rank)...]
    dot_general x7 -> x0, matrix products: 7.54 us -> none  [the longest x3 4.64 us: local_step(): jnp.dot(gram_matrix, basis_cols, precision=lax.Precision.HIGHEST, preferr...]
    another operation x3 -> x0, matrix products: 3.16 us -> none  [local_step(): lax.linalg.triangular_solve(small_factor, power_image, left_side=False, l...]
    unnamed x14 -> x0, local copies, waits for them, and re-layouts: 2.97 us -> none
    mul x1 -> x0, other arithmetic: 1.99 us -> none  [local_step(): normed = (tensor - average[:, None, None]) * inverse_std[:, None, None]]
where the time goes in v2:
time: 66.1 us; the launch traced here: 65.9 us
  Pallas kernels  65.3 us (99%)
    pallas_call x1, Pallas kernels, gram_call(): pl.pallas_call(functools.partial(gram_kernel, sizes, cells), out_shape=(j...  49.3 us
    pallas_call x1, Pallas kernels, basis_call(): pl.pallas_call(basis_kernel, out_shape=(jax.ShapeDtypeStruct((rows, rank)...  16 us

profile of v2, /device:TPU:1, one launch (start us, length us, event | category | flops | bytes accessed | tf_op | source)
XLA Modules:
  0.0 65.9 jit_solution(7261236603435237182)
XLA Ops:
  0.6 49.3 %shard_map.41 = (f32[512,512]{1,0:T(8,128)}, f32[24,128]{1,0:T(8,128)}, bf16[512,1024]{1,0:T(8,128)(2,1)}, bf16[512,1024]{1,0:T(8,128)(2,1)}) custom-call(f32[512,8,128]{2,1,0:T(8,128)} %x_hbm.1), custom_call_target="tpu_custom_call" | custom-call | tf_op jit(solution)/shard_map/pallas_call | solution.py:277
  49.9 16.0 %shard_map.42 = (f32[512,128]{1,0:T(8,128)}, f32[128,8,128]{2,1,0:T(8,128)}) custom-call(f32[512,512]{1,0:T(8,128)} %get-tuple-element.6.gram_ref, f32[24,128]{1,0:T(8,128)} %get-tuple-element.7.stats_ref, f32[512,128]{1,0:T(8,128)} %basis_ref.1, bf16[512,1024]{1,0:T(8,128)(2,1)} %get-tuple-element.8.high_hbm, bf16[512,1024]{1,0:T(8,128)(2,1)} %get-tuple-element.9.low_hbm), custom_call_target="tpu_custom_call" | custom-call | tf_op jit(solution)/shard_map/pallas_call | solution.py:438

commit v3 on v2

--- a/solution.py
+++ b/solution.py
@@ -25,6 +25,18 @@
 
 def near_first(extent):
     return sorted(range(1, extent), key=lambda step: ring_distance(step, extent))
+
+
+def add_up(terms):
+    while len(terms) > 1:
+        pairs = [terms[i] + terms[i + 1] for i in range(0, len(terms) - 1, 2)]
+        terms = pairs + terms[2 * len(pairs):]
+    return terms[0]
+
+
+def split(value):
+    top = value.astype(jnp.bfloat16)
+    return top, (value - top.astype(jnp.float32)).astype(jnp.bfloat16)
 
 
 def dot_nt(left, right, precision=None):
@@ -68,44 +80,44 @@
         copy.start()
         return copy
 
-    load = pltpu.make_async_copy(x_hbm, field, load_sem)
-    load.start()
-    load.wait()
-
-    rows = field.shape[0]
-    slabs = field.shape[1]
+    slabs, rows = field.shape[0], field.shape[1]
     width = float(slabs * BLOCK)
     blocks = rows // BLOCK
+    loads = {}
+    for b in range(blocks):
+        here = pl.ds(b * BLOCK, BLOCK)
+        for s in range(slabs):
+            loads[b, s] = pltpu.make_async_copy(x_hbm.at[here, s, :], field.at[s, here, :], load_sem.at[b, s])
+            loads[b, s].start()
+
     below = lax.broadcasted_iota(jnp.int32, (BLOCK, BLOCK), 0)
     across = lax.broadcasted_iota(jnp.int32, (BLOCK, BLOCK), 1)
     on_diagonal = below == across
 
-    mean_down, mean_over, sums = [], [], []
-    for b in range(blocks):
-        here = pl.ds(b * BLOCK, BLOCK)
-        total = field[here, 0, :]
-        for s in range(1, slabs):
-            total = total + field[here, s, :]
-        total = jnp.broadcast_to(jnp.sum(total, axis=1, keepdims=True), (BLOCK, BLOCK))
-        mean = total * (1.0 / width)
-        for s in range(slabs):
-            centred = field[here, s, :] - mean
-            top = centred.astype(jnp.bfloat16)
-            high[here, pl.ds(s * BLOCK, BLOCK)] = top
-            low[here, pl.ds(s * BLOCK, BLOCK)] = (centred - top.astype(jnp.float32)).astype(jnp.bfloat16)
-        turned = total.T
-        mean_down.append(mean)
-        mean_over.append(turned * (1.0 / width))
-        sums.append(turned[0:1, :])
-
     pair = 2 * BLOCK
-    square = {}
+    mean_down, mean_over, sums, square = [], [], [], {}
     for bi in range(blocks // 2):
+        for b in (2 * bi, 2 * bi + 1):
+            here = pl.ds(b * BLOCK, BLOCK)
+            for s in range(slabs):
+                loads[b, s].wait()
+            total = add_up([field[s, here, :] for s in range(slabs)])
+            total = jnp.broadcast_to(jnp.sum(total, axis=1, keepdims=True), (BLOCK, BLOCK))
+            mean = total * (1.0 / width)
+            for s in range(slabs):
+                top, rest = split(field[s, here, :] - mean)
+                high[here, pl.ds(s * BLOCK, BLOCK)] = top
+                low[here, pl.ds(s * BLOCK, BLOCK)] = rest
+            turned = total.T
+            mean_down.append(mean)
+            mean_over.append(turned * (1.0 / width))
+            sums.append(turned[0:1, :])
         for bj in range(bi + 1):
             left, right = pl.ds(bi * pair, pair), pl.ds(bj * pair, pair)
             value = dot_nt(high[left, :], high[right, :])
-            value = value + dot_nt(high[left, :], low[right, :])
-            value = value + dot_nt(low[left, :], high[right, :])
+            crossed = dot_nt(high[left, :], low[right, :])
+            crossed = crossed + (crossed.T if bi == bj else dot_nt(low[left, :], high[right, :]))
+            value = value + crossed
             for i in range(2):
                 for j in range(2):
                     r, q = 2 * bi + i, 2 * bj + j
@@ -282,10 +294,10 @@
             jax.ShapeDtypeStruct((rows, slabs * lanes), bf16),
             jax.ShapeDtypeStruct((rows, slabs * lanes), bf16),
         ),
-        in_specs=[pl.BlockSpec(memory_space=pl.ANY)],
+        in_specs=[pl.BlockSpec(memory_space=pltpu.HBM)],
         out_specs=(pl.BlockSpec(memory_space=pltpu.VMEM),) * 4,
         scratch_shapes=[
-            vmem((rows, slabs, lanes), f32),
+            vmem((slabs, rows, lanes), f32),
             vmem((2, nx, tiles_x + 1, 8, lanes), f32),
             vmem((nx, tiles_x + 1, 8, lanes), f32),
             vmem((nx - 1, tiles_x + 1, 8, lanes), f32),
@@ -294,7 +306,7 @@
             vmem((nz, tiles_z + 1, 8, lanes), f32),
             vmem((ny, tiles_z + 1, 8, lanes), f32),
             vmem((128, 8, lanes), f32),
-            dma,
+            dma((rows // BLOCK, slabs)),
             dma((nx,)), dma((nx,)),
             dma((nx - 1,)), dma((nx - 1,)),
             dma((nz - 1,)), dma((nz - 1,)),
@@ -303,93 +315,115 @@
             dma((nx - 1, nz)), dma((nx - 1, nz)),
             dma((nx, nz)), dma((nx, nz)),
         ],
-        compiler_params=pltpu.CompilerParams(collective_id=0, has_side_effects=True),
-    )(tensor)
-
-
-def over(value, lane, one):
-    return jnp.broadcast_to(value[:, lane:lane + 1], (8, BLOCK)) * one
+        compiler_params=pltpu.CompilerParams(
+            collective_id=0, has_side_effects=True, vmem_limit_bytes=16 << 20
+        ),
+    )(pltpu.with_memory_space_constraint(tensor, pltpu.HBM))
+
+
+def over(value, lane):
+    return jnp.broadcast_to(value[:, lane:lane + 1], (8, BLOCK))
 
 
 def down(value, line):
     return jnp.broadcast_to(value[line:line + 1, :], (8, BLOCK))
 
 
-def add_up(terms):
-    while len(terms) > 1:
-        terms = [terms[i] + terms[i + 1] for i in range(0, len(terms), 2)]
-    return terms[0]
-
-
-def inverse_factor(matrix, one):
-    groups = BLOCK // 8
+def eliminate(a, base, one):
+    groups = len(a)
+    a = list(a)
     line = lax.broadcasted_iota(jnp.int32, (8, BLOCK), 0)
     lane = lax.broadcasted_iota(jnp.int32, (8, BLOCK), 1)
-    a = [matrix[8 * v:8 * v + 8, :] for v in range(groups)]
-    w = [jnp.where(lane == line + 8 * v, 1.0, 0.0).astype(jnp.float32) for v in range(groups)]
+
+    def spread(v, first):
+        columns = [over(a[v], first + m) for m in range(8)]
+        return [columns[0] * one, columns[1] * one] + columns[2:]
+
     result = []
-    panel = [over(a[0], m, one) for m in range(8)]
-    under = [over(a[1], m, one) for m in range(8)]
+    panel, under = spread(0, base), spread(1, base)
     for v0 in range(groups):
-        first = 8 * v0
+        first = base + 8 * v0
         more = v0 + 1 < groups
+        inside = (lane >= first) & (lane < first + 8)
         if more:
-            ahead = [over(a[v0 + 1], first + 8 + m, one) for m in range(8)]
-            spread = [under] + [
-                [over(a[v], first + m, one) for m in range(8)] for v in range(v0 + 2, groups)
-            ]
+            ahead = [over(a[v0 + 1], first + 8 + m) for m in range(8)]
+            columns = [under] + [[over(a[v], first + m) for m in range(8)] for v in range(v0 + 2, groups)]
             rest = list(under)
-        row_a, row_w = a[v0], w[v0]
-        ratios = []
-        for j in range(8):
-            pivot = down(panel[j], j)
-            reciprocal = 1.0 / pivot
-            pivots = pivot if j == 0 else jnp.where(line == j, pivot, pivots)
-            reciprocals = reciprocal if j == 0 else jnp.where(line == j, reciprocal, reciprocals)
+        rows = jnp.where(inside, jnp.where(lane == line + first, 1.0, 0.0).astype(jnp.float32), a[v0])
+        ratios, pivots = [None] * 8, {}
+        for j in range(0, 8, 2):
+            p, q, r = down(panel[j], j), down(panel[j], j + 1), down(panel[j + 1], j + 1)
+            determinant = p * r - q * q
+            inverse = 1.0 / determinant
+            pi, qi, ri = p * inverse, q * inverse, r * inverse
+            pivots[j] = (p, q, r, pi, qi, ri, determinant)
             if more:
-                ratios.append(rest[j] * reciprocal)
-            if j < 7:
-                ratio = jnp.where(line > j, panel[j] * reciprocal, 0.0)
-                for m in range(j + 1, 8):
-                    entry = down(panel[m], j)
-                    panel[m] = panel[m] - ratio * entry
+                ratios[j] = rest[j] * ri - rest[j + 1] * qi
+                ratios[j + 1] = rest[j + 1] * pi - rest[j] * qi
+            if j < 6:
+                left = jnp.where(line > j + 1, panel[j] * ri - panel[j + 1] * qi, 0.0)
+                right = jnp.where(line > j + 1, panel[j + 1] * pi - panel[j] * qi, 0.0)
+                for m in range(j + 2, 8):
+                    upper, lower = down(panel[m], j), down(panel[m], j + 1)
+                    panel[m] = panel[m] - (left * upper + right * lower)
                     if more:
-                        rest[m] = rest[m] - ratios[j] * entry
-                row_a = row_a - ratio * down(row_a, j)
-                row_w = row_w - ratio * down(row_w, j)
-        result.append(row_w * lax.rsqrt(pivots))
+                        rest[m] = rest[m] - (ratios[j] * upper + ratios[j + 1] * lower)
+                rows = rows - (left * down(rows, j) + right * down(rows, j + 1))
+        scaled, solved = rows, []
+        for j in range(0, 8, 2):
+            p, q, r, pi, qi, ri, determinant = pivots[j]
+            upper, lower = down(rows, j), down(rows, j + 1)
+            root = lax.rsqrt(p)
+            square = root * root
+            scaled = jnp.where(line == j, upper * root, scaled)
+            scaled = jnp.where(
+                line == j + 1, (lower - q * square * upper) * lax.rsqrt(determinant * square), scaled
+            )
+            solved.append((ri * upper - qi * lower, pi * lower - qi * upper))
+        result.append(scaled)
         if more:
             following = [
                 ahead[m] - add_up([ratios[j] * down(rest[j], m) for j in range(8)]) for m in range(8)
             ]
-            row_a, row_w = row_a * reciprocals, row_w * reciprocals
-            for j in range(7, 0, -1):
-                ratio = jnp.where(line < j, panel[j] * reciprocals, 0.0)
-                row_a = row_a - ratio * down(row_a, j)
-                row_w = row_w - ratio * down(row_w, j)
-            from_a = [down(row_a, m) for m in range(8)]
-            from_w = [down(row_w, m) for m in range(8)]
+            change = [None] * 8
+            for j in range(6, -1, -2):
+                upper, lower = solved[j // 2]
+                if j < 6:
+                    p, q, r, pi, qi, ri, determinant = pivots[j]
+                    first_sum = add_up([down(panel[m], j) * change[m] for m in range(j + 2, 8)])
+                    second_sum = add_up([down(panel[m], j + 1) * change[m] for m in range(j + 2, 8)])
+                    upper = upper - (ri * first_sum - qi * second_sum)
+                    lower = lower - (pi * second_sum - qi * first_sum)
+                change[j], change[j + 1] = upper, lower
             for index, v in enumerate(range(v0 + 1, groups)):
-                a[v] = a[v] - add_up([spread[index][m] * from_a[m] for m in range(8)])
-                w[v] = w[v] - add_up([spread[index][m] * from_w[m] for m in range(8)])
+                a[v] = jnp.where(inside, 0.0, a[v]) - add_up([columns[index][m] * change[m] for m in range(8)])
             panel = following
             if v0 + 2 < groups:
-                under = [over(a[v0 + 2], first + 8 + m, one) for m in range(8)]
+                under = spread(v0 + 2, first + 8)
     return result
 
 
-def split(value):
-    top = value.astype(jnp.bfloat16)
-    return top, (value - top.astype(jnp.float32)).astype(jnp.bfloat16)
-
-
-def basis_kernel(gram_ref, stats_ref, basis_ref, high_hbm, low_hbm, factor_ref, core_ref, high, low, turned, image, inverse, sems):
-    loads = [
-        pltpu.make_async_copy(high_hbm, high, sems.at[0]),
-        pltpu.make_async_copy(low_hbm, low, sems.at[1]),
+def inverse_factor(matrix, one):
+    lane = lax.broadcasted_iota(jnp.int32, (8, BLOCK), 1)
+    half = BLOCK // 2
+    groups = [matrix[8 * v:8 * v + 8, :] for v in range(BLOCK // 8)]
+    top = eliminate(groups[:8], 0, one)
+    top = [jnp.where((lane < 8 * v + 8) | (lane >= half), rows, 0.0) for v, rows in enumerate(top)]
+    beyond = [jnp.where(lane >= half, rows, 0.0) for rows in top]
+    change = lax.dot_general(
+        jnp.concatenate(beyond, axis=0), jnp.concatenate(top, axis=0), (((0,), (0,)), ((), ())),
+        precision=lax.Precision.HIGHEST, preferred_element_type=jnp.float32,
+    )
+    bottom = [
+        jnp.where(lane >= half, rows, 0.0) - change[half + 8 * v:half + 8 * v + 8, :]
+        for v, rows in enumerate(groups[8:])
     ]
-    for load in loads:
-        load.start()
+    bottom = eliminate(bottom, half, one)
+    bottom = [jnp.where(lane < half + 8 * v + 8, rows, 0.0) for v, rows in enumerate(bottom)]
+    return [jnp.where(lane < half, rows, 0.0) for rows in top] + bottom
+
+
+def basis_kernel(gram_ref, stats_ref, basis_ref, high, low, factor_ref, core_ref, turned, image, inverse):
     rows, rank = basis_ref.shape
     blocks = rows // BLOCK
     highest = lax.Precision.HIGHEST
@@ -418,8 +452,6 @@
         constant = term if constant is None else constant + term
     constant = jnp.broadcast_to(jnp.sum(constant, axis=1, keepdims=True), (rank, BLOCK))
     top, rest = split(image[...])
-    for load in loads:
-        load.wait()
     slabs = core_ref.shape[1]
     for s in range(0, slabs, 2):
         window = pl.ds(s * BLOCK, 2 * BLOCK)
@@ -432,25 +464,22 @@
 
 def basis_call(gram_matrix, stats, basis, high, low, slabs):
     rows, rank = basis.shape
-    f32, bf16 = jnp.float32, jnp.bfloat16
+    f32 = jnp.float32
     vmem = pl.BlockSpec(memory_space=pltpu.VMEM)
-    hbm = pl.BlockSpec(memory_space=pl.ANY)
     return pl.pallas_call(
         basis_kernel,
         out_shape=(
             jax.ShapeDtypeStruct((rows, rank), f32),
             jax.ShapeDtypeStruct((rank, slabs, BLOCK), f32),
         ),
-        in_specs=[vmem, vmem, vmem, hbm, hbm],
+        in_specs=[vmem] * 5,
         out_specs=(vmem, vmem),
         scratch_shapes=[
-            pltpu.VMEM(high.shape, bf16),
-            pltpu.VMEM(low.shape, bf16),
             pltpu.VMEM((rank, rows), f32),
             pltpu.VMEM((rank, rows), f32),
             pltpu.VMEM((rank, rank), f32),
-            pltpu.SemaphoreType.DMA((2,)),
         ],
+        compiler_params=pltpu.CompilerParams(vmem_limit_bytes=16 << 20),
     )(gram_matrix, stats, basis, high, low)
 
 

time: 66.1 us -> 61 us (0.923)
  Pallas kernels: 65.3 us -> 60.2 us
    pallas_call x1, Pallas kernels: 49.3 us -> 46.4 us  [gram_call(): pl.pallas_call(functools.partial(gram_kernel, sizes, cells), out_shape=(j...]
    pallas_call x1, Pallas kernels: 16 us -> 13.7 us  [basis_call(): pl.pallas_call(basis_kernel, out_shape=(jax.ShapeDtypeStruct((rows, rank)...]
where the time goes in v3:
time: 61 us; the launch traced here: 60.8 us
  Pallas kernels  60.2 us (99%)
  between operations  0.65 us (1%)
    pallas_call x1, Pallas kernels, gram_call(): pl.pallas_call(functools.partial(gram_kernel, sizes, cells), out_shape=(j...  46.4 us
    pallas_call x1, Pallas kernels, basis_call(): pl.pallas_call(basis_kernel, out_shape=(jax.ShapeDtypeStruct((rows, rank)...  13.7 us

profile of v3, /device:TPU:1, one launch (start us, length us, event | category | flops | bytes accessed | tf_op | source)
XLA Modules:
  0.0 60.8 jit_solution(7662607285094379381)
XLA Ops:
  0.6 0.0 copy-start
  0.6 46.4 %shard_map.41 = (f32[512,512]{1,0:T(8,128)S(1)}, f32[24,128]{1,0:T(8,128)S(1)}, bf16[512,1024]{1,0:T(8,128)(2,1)S(1)}, bf16[512,1024]{1,0:T(8,128)(2,1)S(1)}) custom-call(f32[512,8,128]{2,1,0:T(8,128)} %x_hbm.1), custom_call_target="tpu_custom_call" | custom-call | tf_op jit(solution)/shard_map/pallas_call | solution.py:289
  47.1 0.0 copy-done
  47.1 13.7 %shard_map.42 = (f32[512,128]{1,0:T(8,128)}, f32[128,8,128]{2,1,0:T(8,128)}) custom-call(f32[512,512]{1,0:T(8,128)S(1)} %get-tuple-element.6.gram_ref, f32[24,128]{1,0:T(8,128)S(1)} %get-tuple-element.7.stats_ref, f32[512,128]{1,0:T(8,128)S(1)} %copy-done, bf16[512,1024]{1,0:T(8,128)(2,1)S(1)} %get-tuple-element.8.high, ...), custom_call_target="tpu_custom_call" | custom-call | tf_op jit(solution)/shard_map/pallas_call | solution.py:469
Async XLA Ops:
  0.6 46.5 %copy-start = (f32[512,128]{1,0:T(8,128)S(1)}, f32[512,128]{1,0:T(8,128)}, u32[]{:S(2)}) copy-start(f32[512,128]{1,0:T(8,128)} %basis_ref.1) | copy-start | bytes 786436

commit v4 on v3

--- a/solution.py
+++ b/solution.py
@@ -149,16 +149,12 @@
     order_x = far_first(nx) + [0]
     partner = device(other=True)
     sent = []
-    core_copies = {}
-    for d in order_x:
-        core_copies[d] = send(
-            local.at[1 - core, lax.rem(x + d, nx)], from_core.at[d], core_send.at[d], core_recv.at[d], partner
-        )
-    sent += list(core_copies.values())
+    whole_half = send(local.at[1 - core], from_core, core_send.at[0], core_recv.at[0], partner)
+    sent.append(whole_half)
+    whole_half.wait_recv()
     x_copies = {}
     for d in order_x:
-        core_copies[d].wait_recv()
-        value = local[core, lax.rem(x + d, nx)] + from_core[d]
+        value = local[core, lax.rem(x + d, nx)] + from_core[lax.rem(x + d, nx)]
         if d == 0:
             from_x[0] = value
         else:
@@ -214,25 +210,16 @@
     for d in far_first(nz):
         gz[d] = send(mine, mine, gz_send.at[d - 1], gz_recv.at[d - 1], device(dz=d))
 
-    def pass_on(dx, dz):
-        piece = place(dx, dz)
-        if dx == 0:
-            for d in far_first(nx):
-                gx[d, dz] = send(piece, piece, gx_send.at[d - 1, dz], gx_recv.at[d - 1, dz], device(dx=d))
-        gc[dx, dz] = send(piece, piece, gc_send.at[dx, dz], gc_recv.at[dx, dz], partner)
-
-    pass_on(0, 0)
-    arrivals = [(1.0 + ring_distance(d, nz), 0, d) for d in range(1, nz)]
-    arrivals += [
-        ((1.0 + ring_distance(d, nz) if d else 0.0) + 1.0 + ring_distance(e, nx), e, d)
-        for e in range(1, nx) for d in range(nz)
-    ]
-    for _, e, d in sorted(arrivals):
-        if e == 0:
-            gz[d].wait_recv()
-        else:
-            gx[e, d].wait_recv()
-        pass_on(e, d)
+    for d in near_first(nz):
+        gz[d].wait_recv()
+    def square_at(dx):
+        return packed.at[pl.ds(64 * core + tiles_x * lax.rem(x + nx - dx, nx), tiles_x)]
+    for d in far_first(nx):
+        gx[d] = send(square_at(0), square_at(0), gx_send.at[d - 1, 0], gx_recv.at[d - 1, 0], device(dx=d))
+    gc[0] = send(square_at(0), square_at(0), gc_send.at[0, 0], gc_recv.at[0, 0], partner)
+    for d in near_first(nx):
+        gx[d].wait_recv()
+        gc[d] = send(square_at(d), square_at(d), gc_send.at[d, 0], gc_recv.at[d, 0], partner)
     for copy in gc.values():
         copy.wait_recv()
 
@@ -329,7 +316,7 @@
     return jnp.broadcast_to(value[line:line + 1, :], (8, BLOCK))
 
 
-def eliminate(a, base, one):
+def eliminate(a, base, one, aside=()):
     groups = len(a)
     a = list(a)
     line = lax.broadcasted_iota(jnp.int32, (8, BLOCK), 0)
@@ -342,6 +329,8 @@
     result = []
     panel, under = spread(0, base), spread(1, base)
     for v0 in range(groups):
+        if v0 < len(aside):
+            aside[v0]()
         first = base + 8 * v0
         more = v0 + 1 < groups
         inside = (lane >= first) & (lane < first + 8)
@@ -403,11 +392,11 @@
     return result
 
 
-def inverse_factor(matrix, one):
+def inverse_factor(matrix, one, aside=()):
     lane = lax.broadcasted_iota(jnp.int32, (8, BLOCK), 1)
     half = BLOCK // 2
     groups = [matrix[8 * v:8 * v + 8, :] for v in range(BLOCK // 8)]
-    top = eliminate(groups[:8], 0, one)
+    top = eliminate(groups[:8], 0, one, aside[:8])
     top = [jnp.where((lane < 8 * v + 8) | (lane >= half), rows, 0.0) for v, rows in enumerate(top)]
     beyond = [jnp.where(lane >= half, rows, 0.0) for rows in top]
     change = lax.dot_general(
@@ -418,7 +407,7 @@
         jnp.where(lane >= half, rows, 0.0) - change[half + 8 * v:half + 8 * v + 8, :]
         for v, rows in enumerate(groups[8:])
     ]
-    bottom = eliminate(bottom, half, one)
+    bottom = eliminate(bottom, half, one, aside[8:])
     bottom = [jnp.where(lane < half + 8 * v + 8, rows, 0.0) for v, rows in enumerate(bottom)]
     return [jnp.where(lane < half, rows, 0.0) for rows in top] + bottom
 
@@ -431,15 +420,26 @@
         turned[:, b * BLOCK:(b + 1) * BLOCK] = basis_ref[pl.ds(b * BLOCK, BLOCK), :].T
     one = stats_ref[16:24, :]
 
+    def orthonormal(target, aside=()):
+        small = dot_nt(image[...], image[...], precision=highest)
+        for v, group in enumerate(inverse_factor(small, one, aside)):
+            inverse[pl.ds(8 * v, 8), :] = group
+        return jnp.dot(inverse[...], target[...], precision=highest, preferred_element_type=jnp.float32)
+
     def body(iteration, carry):
-        image[...] = jnp.dot(turned[...], gram_ref[...], precision=highest, preferred_element_type=jnp.float32)
-        small = dot_nt(image[...], image[...], precision=highest)
-        for v, group in enumerate(inverse_factor(small, one)):
-            inverse[pl.ds(8 * v, 8), :] = group
-        turned[...] = jnp.dot(inverse[...], image[...], precision=highest, preferred_element_type=jnp.float32)
+        def chunk(part):
+            window = pl.ds(256 * part, 256)
+            turned[:, window] = jnp.dot(
+                image[...], gram_ref[:, window], precision=highest, preferred_element_type=jnp.float32
+            )
+
+        todo = [functools.partial(chunk, part) for part in range(2)]
+        image[...] = orthonormal(turned, [todo[v // 8] if v % 8 == 0 else (lambda: None) for v in range(16)])
         return carry
 
-    lax.fori_loop(0, ITERS, body, 0)
+    image[...] = jnp.dot(turned[...], gram_ref[...], precision=highest, preferred_element_type=jnp.float32)
+    lax.fori_loop(0, ITERS - 1, body, 0)
+    turned[...] = orthonormal(image)
 
     constant = None
     for b in range(blocks):

time: 61 us -> 57.7 us (0.946)
  Pallas kernels: 60.2 us -> 56.9 us
    pallas_call x1, Pallas kernels: 46.4 us -> 44.5 us  [gram_call(): pl.pallas_call(functools.partial(gram_kernel, sizes, cells), out_shape=(j...]
    pallas_call x1, Pallas kernels: 13.7 us -> 12.3 us  [basis_call(): pl.pallas_call(basis_kernel, out_shape=(jax.ShapeDtypeStruct((rows, rank)...]
where the time goes in v4:
time: 57.7 us; the launch traced here: 57.6 us
  Pallas kernels  56.9 us (99%)
  between operations  0.65 us (1%)
    pallas_call x1, Pallas kernels, gram_call(): pl.pallas_call(functools.partial(gram_kernel, sizes, cells), out_shape=(j...  44.5 us
    pallas_call x1, Pallas kernels, basis_call(): pl.pallas_call(basis_kernel, out_shape=(jax.ShapeDtypeStruct((rows, rank)...  12.3 us

profile of v4, /device:TPU:1, one launch (start us, length us, event | category | flops | bytes accessed | tf_op | source)
XLA Modules:
  0.0 57.6 jit_solution(15134297440546697825)
XLA Ops:
  0.6 0.0 copy-start
  0.6 44.5 %shard_map.41 = (f32[512,512]{1,0:T(8,128)S(1)}, f32[24,128]{1,0:T(8,128)S(1)}, bf16[512,1024]{1,0:T(8,128)(2,1)S(1)}, bf16[512,1024]{1,0:T(8,128)(2,1)S(1)}) custom-call(f32[512,8,128]{2,1,0:T(8,128)} %x_hbm.1), custom_call_target="tpu_custom_call" | custom-call | tf_op jit(solution)/shard_map/pallas_call | solution.py:276
  45.2 0.0 copy-done
  45.2 12.3 %shard_map.42 = (f32[512,128]{1,0:T(8,128)}, f32[128,8,128]{2,1,0:T(8,128)}) custom-call(f32[512,512]{1,0:T(8,128)S(1)} %get-tuple-element.6.gram_ref, f32[24,128]{1,0:T(8,128)S(1)} %get-tuple-element.7.stats_ref, f32[512,128]{1,0:T(8,128)S(1)} %copy-done, bf16[512,1024]{1,0:T(8,128)(2,1)S(1)} %get-tuple-element.8.high, ...), custom_call_target="tpu_custom_call" | custom-call | tf_op jit(solution)/shard_map/pallas_call | solution.py:469
Async XLA Ops:
  0.6 44.6 %copy-start = (f32[512,128]{1,0:T(8,128)S(1)}, f32[512,128]{1,0:T(8,128)}, u32[]{:S(2)}) copy-start(f32[512,128]{1,0:T(8,128)} %basis_ref.1) | copy-start | bytes 786436

commit v5 on v4

--- a/solution.py
+++ b/solution.py
@@ -48,7 +48,7 @@
 def gram_kernel(
     sizes, cells,
     x_hbm, gram_ref, stats_ref, high, low,
-    field, local, from_core, to_x, from_x, to_z, from_z, from_y, packed,
+    field, local, from_core, to_x, from_x, to_z, from_z, from_y, packed, across_ref, down_ref,
     load_sem, core_send, core_recv, x_send, x_recv, z_send, z_recv, y_send, y_recv,
     gz_send, gz_recv, gx_send, gx_recv, gc_send, gc_recv,
 ):
@@ -64,10 +64,10 @@
         to_col = lax.rem(z + dz, nz) * 2 + (1 - core if other else core)
         return (to_row, to_col)
 
-    peers = [device(other=True)]
-    peers += [device(dx=d) for d in range(1, nx)]
-    peers += [device(dz=d) for d in range(1, nz)]
-    peers += [device(dy=d) for d in range(1, ny)]
+    reach = [(-ring_distance(d, nz), device(dz=d)) for d in range(1, nz)]
+    reach += [(-ring_distance(d, ny), device(dy=d)) for d in range(1, ny)]
+    reach += [(-ring_distance(d, nx), device(dx=d)) for d in range(1, nx)]
+    peers = [peer for _, peer in sorted(reach, key=lambda entry: entry[0])] + [device(other=True)]
     barrier = pltpu.get_barrier_semaphore()
     for peer in peers:
         pl.semaphore_signal(barrier, inc=1, device_id=peer, device_id_type=MESH)
@@ -130,7 +130,7 @@
         return jnp.sum(jnp.where(on_diagonal, block, 0.0), axis=0, keepdims=True)
 
     extra = jnp.concatenate(
-        sums + [diagonal_of(square[0, 0]), diagonal_of(square[2, 2]), jnp.zeros((2, BLOCK), jnp.float32)], axis=0
+        sums + [diagonal_of(square[b, b]) for b in range(blocks)], axis=0
     )
     for index, (r, q) in enumerate(SQUARES):
         half, slot = index // 4, (index % 4) * 16
@@ -210,56 +210,61 @@
     for d in far_first(nz):
         gz[d] = send(mine, mine, gz_send.at[d - 1], gz_recv.at[d - 1], device(dz=d))
 
-    for d in near_first(nz):
-        gz[d].wait_recv()
-    def square_at(dx):
-        return packed.at[pl.ds(64 * core + tiles_x * lax.rem(x + nx - dx, nx), tiles_x)]
-    for d in far_first(nx):
-        gx[d] = send(square_at(0), square_at(0), gx_send.at[d - 1, 0], gx_recv.at[d - 1, 0], device(dx=d))
-    gc[0] = send(square_at(0), square_at(0), gc_send.at[0, 0], gc_recv.at[0, 0], partner)
-    for d in near_first(nx):
-        gx[d].wait_recv()
-        gc[d] = send(square_at(d), square_at(d), gc_send.at[d, 0], gc_recv.at[d, 0], partner)
-    for copy in gc.values():
-        copy.wait_recv()
-
-    means, scales, seconds = [], [], []
-    def matrix(index):
-        return packed[pl.ds(16 * index, 16)].reshape(BLOCK, BLOCK)
-
-    whole = {}
-    for index, (r, q) in enumerate(SQUARES):
-        block = matrix(index)
-        if index in PAIRED:
-            first, second = min(r, q), max(r, q)
-            turned = block.T
-            line = extra[4 + first // 2:5 + first // 2, :]
-            whole[first, first] = jnp.where(
-                below > across, block, jnp.where(below < across, turned, jnp.broadcast_to(line, (BLOCK, BLOCK)))
-            )
-            whole[second, second] = jnp.where(below <= across, block, turned)
-        else:
-            whole[r, q] = block
+    def turn(line):
+        return jnp.broadcast_to(line, (BLOCK, BLOCK)).T
+
     for b in range(blocks):
         average = extra[b:b + 1, :] / cells
-        if b % 2 == 0:
-            second = extra[4 + b // 2:5 + b // 2, :]
-        else:
-            second = diagonal_of(whole[b, b])
-        scale = 1.0 / jnp.sqrt(second / cells - average * average + 1e-05)
+        scale = 1.0 / jnp.sqrt(extra[4 + b:5 + b, :] / cells - average * average + 1e-05)
         stats_ref[b:b + 1, :] = average
         stats_ref[4 + b:5 + b, :] = scale
         stats_ref[8 + b:9 + b, :] = sums[b] * (1.0 / width) - average
-        means.append(jnp.broadcast_to(average, (BLOCK, BLOCK)))
-        scales.append(jnp.broadcast_to(scale, (BLOCK, BLOCK)))
+        across_ref[0, b] = jnp.broadcast_to(scale * (1.0 / cells), (8, BLOCK))
+        across_ref[1, b] = jnp.broadcast_to(scale * average, (8, BLOCK))
+        across_ref[2, b] = jnp.broadcast_to(extra[4 + b:5 + b, :], (8, BLOCK))
+        down_ref[0, b] = turn(scale)
+        down_ref[1, b] = turn(scale * average)
     stats_ref[16:24, :] = jnp.ones((8, BLOCK), jnp.float32)
-    means_down = [value.T for value in means]
-    scales_down = [value.T for value in scales]
-    for (r, q), block in whole.items():
-        value = (block * (1.0 / cells) - means_down[r] * means[q]) * scales_down[r] * scales[q]
-        gram_ref[pl.ds(r * BLOCK, BLOCK), pl.ds(q * BLOCK, BLOCK)] = value
-        if r != q:
-            gram_ref[pl.ds(q * BLOCK, BLOCK), pl.ds(r * BLOCK, BLOCK)] = value.T
+
+    for d in near_first(nz):
+        gz[d].wait_recv()
+
+    def square_at(dx):
+        return packed.at[pl.ds(64 * core + tiles_x * lax.rem(x + nx - dx, nx), tiles_x)]
+
+    for d in far_first(nx):
+        gx[d] = send(square_at(0), square_at(0), gx_send.at[d - 1], gx_recv.at[d - 1], device(dx=d))
+    gc[0] = send(square_at(0), square_at(0), gc_send.at[0], gc_recv.at[0], partner)
+    for d in near_first(nx):
+        gx[d].wait_recv()
+        gc[d] = send(square_at(d), square_at(d), gc_send.at[d], gc_recv.at[d], partner)
+
+    def spot(block_index):
+        return pl.ds(pl.multiple_of(block_index * BLOCK, BLOCK), BLOCK)
+
+    def put(block, r, q, mirror):
+        value = block * (down_ref[0, r] * across_ref[0, q][0:1, :]) - down_ref[1, r] * across_ref[1, q][0:1, :]
+        gram_ref[spot(r), spot(q)] = value
+        if mirror:
+            gram_ref[spot(q), spot(r)] = value.T
+
+    def unpack(half):
+        for slot in range(4):
+            block = packed[pl.ds(64 * half + 16 * slot, 16)].reshape(BLOCK, BLOCK)
+            (r, q), (later_r, later_q) = SQUARES[slot], SQUARES[4 + slot]
+            r, q = r + half * (later_r - r), q + half * (later_q - q)
+            if slot in PAIRED:
+                turned = block.T
+                line = jnp.broadcast_to(across_ref[2, r][0:1, :], (BLOCK, BLOCK))
+                put(jnp.where(below > across, block, jnp.where(below < across, turned, line)), r, r, False)
+                put(jnp.where(below <= across, block, turned), q, q, False)
+            else:
+                put(block, r, q, True)
+
+    unpack(core)
+    for copy in gc.values():
+        copy.wait_recv()
+    unpack(1 - core)
 
     for copy in sent + list(gz.values()) + list(gx.values()) + list(gc.values()):
         copy.wait_send()
@@ -293,14 +298,16 @@
             vmem((nz, tiles_z + 1, 8, lanes), f32),
             vmem((ny, tiles_z + 1, 8, lanes), f32),
             vmem((128, 8, lanes), f32),
+            vmem((3, rows // BLOCK, 8, lanes), f32),
+            vmem((2, rows // BLOCK, BLOCK, lanes), f32),
             dma((rows // BLOCK, slabs)),
             dma((nx,)), dma((nx,)),
             dma((nx - 1,)), dma((nx - 1,)),
             dma((nz - 1,)), dma((nz - 1,)),
             dma((ny - 1,)), dma((ny - 1,)),
             dma((nz - 1,)), dma((nz - 1,)),
-            dma((nx - 1, nz)), dma((nx - 1, nz)),
-            dma((nx, nz)), dma((nx, nz)),
+            dma((nx - 1,)), dma((nx - 1,)),
+            dma((nx,)), dma((nx,)),
         ],
         compiler_params=pltpu.CompilerParams(
             collective_id=0, has_side_effects=True, vmem_limit_bytes=16 << 20
@@ -412,7 +419,9 @@
     return [jnp.where(lane < half, rows, 0.0) for rows in top] + bottom
 
 
-def basis_kernel(gram_ref, stats_ref, basis_ref, high, low, factor_ref, core_ref, turned, image, inverse):
+def basis_kernel(
+    gram_ref, stats_ref, basis_ref, high, low, factor_hbm, core_hbm, turned, image, inverse, factor_ref, core_ref, sems
+):
     rows, rank = basis_ref.shape
     blocks = rows // BLOCK
     highest = lax.Precision.HIGHEST
@@ -450,16 +459,23 @@
         image[:, window] = value
         term = value * stats_ref[8 + b:9 + b, :]
         constant = term if constant is None else constant + term
+    slabs = core_ref.shape[0]
+    stores = [pltpu.make_async_copy(factor_ref, factor_hbm, sems.at[slabs])]
+    stores[0].start()
     constant = jnp.broadcast_to(jnp.sum(constant, axis=1, keepdims=True), (rank, BLOCK))
     top, rest = split(image[...])
-    slabs = core_ref.shape[1]
     for s in range(0, slabs, 2):
         window = pl.ds(s * BLOCK, 2 * BLOCK)
         value = jnp.dot(top, high[:, window], preferred_element_type=jnp.float32)
         value = value + jnp.dot(top, low[:, window], preferred_element_type=jnp.float32)
         value = value + jnp.dot(rest, high[:, window], preferred_element_type=jnp.float32)
-        core_ref[:, s, :] = value[:, :BLOCK] + constant
-        core_ref[:, s + 1, :] = value[:, BLOCK:] + constant
+        core_ref[s] = value[:, :BLOCK] + constant
+        core_ref[s + 1] = value[:, BLOCK:] + constant
+        for slab in (s, s + 1):
+            stores.append(pltpu.make_async_copy(core_ref.at[slab], core_hbm.at[:, slab, :], sems.at[slab]))
+            stores[-1].start()
+    for store in stores:
+        store.wait()
 
 
 def basis_call(gram_matrix, stats, basis, high, low, slabs):
@@ -473,11 +489,14 @@
             jax.ShapeDtypeStruct((rank, slabs, BLOCK), f32),
         ),
         in_specs=[vmem] * 5,
-        out_specs=(vmem, vmem),
+        out_specs=(pl.BlockSpec(memory_space=pl.ANY),) * 2,
         scratch_shapes=[
             pltpu.VMEM((rank, rows), f32),
             pltpu.VMEM((rank, rows), f32),
             pltpu.VMEM((rank, rank), f32),
+            pltpu.VMEM((rows, rank), f32),
+            pltpu.VMEM((slabs, rank, BLOCK), f32),
+            pltpu.SemaphoreType.DMA((slabs + 1,)),
         ],
         compiler_params=pltpu.CompilerParams(vmem_limit_bytes=16 << 20),
     )(gram_matrix, stats, basis, high, low)

time: 57.7 us -> 56.2 us (0.974)
  Pallas kernels: 56.9 us -> 55.4 us
    pallas_call x1, Pallas kernels: 44.5 us -> 43.3 us  [gram_call(): pl.pallas_call(functools.partial(gram_kernel, sizes, cells), out_shape=(j...]
where the time goes in v5:
time: 56.2 us; the launch traced here: 56 us
  Pallas kernels  55.4 us (99%)
  between operations  0.65 us (1%)
    pallas_call x1, Pallas kernels, gram_call(): pl.pallas_call(functools.partial(gram_kernel, sizes, cells), out_shape=(j...  43.3 us
    pallas_call x1, Pallas kernels, basis_call(): pl.pallas_call(basis_kernel, out_shape=(jax.ShapeDtypeStruct((rows, rank)...  12.1 us

profile of v5, /device:TPU:1, one launch (start us, length us, event | category | flops | bytes accessed | tf_op | source)
XLA Modules:
  0.0 56.0 jit_solution(10792653902271677625)
XLA Ops:
  0.6 0.0 copy-start
  0.6 43.3 %shard_map.41 = (f32[512,512]{1,0:T(8,128)S(1)}, f32[24,128]{1,0:T(8,128)S(1)}, bf16[512,1024]{1,0:T(8,128)(2,1)S(1)}, bf16[512,1024]{1,0:T(8,128)(2,1)S(1)}) custom-call(f32[512,8,128]{2,1,0:T(8,128)} %x_hbm.1), custom_call_target="tpu_custom_call" | custom-call | tf_op jit(solution)/shard_map/pallas_call | solution.py:281
  43.9 0.0 copy-done
  43.9 12.1 %shard_map.42 = (f32[512,128]{1,0:T(8,128)}, f32[128,8,128]{2,1,0:T(8,128)}) custom-call(f32[512,512]{1,0:T(8,128)S(1)} %get-tuple-element.6.gram_ref, f32[24,128]{1,0:T(8,128)S(1)} %get-tuple-element.7.stats_ref, f32[512,128]{1,0:T(8,128)S(1)} %copy-done, bf16[512,1024]{1,0:T(8,128)(2,1)S(1)} %get-tuple-element.8.high, ...), custom_call_target="tpu_custom_call" | custom-call | tf_op jit(solution)/shard_map/pallas_call | solution.py:485
Async XLA Ops:
  0.6 43.3 %copy-start = (f32[512,128]{1,0:T(8,128)S(1)}, f32[512,128]{1,0:T(8,128)}, u32[]{:S(2)}) copy-start(f32[512,128]{1,0:T(8,128)} %basis_ref.1) | copy-start | bytes 786436
